TPU v7x, 256 devices: a whole 4x4x8 slice. The times are simulated.
256 devices in a mesh: ctx: 32 (over x, z), head: 8 (over y, core).
Axes of the slice: x: 4, y: 4, z: 8, core: 2. Of those that a mesh axis runs over, the one named last changes fastest.
Arguments:
- queries: float32 [32768, 768], P(('ctx', 'head')), may hold values from -280 to 280, as said below
- keys: float32 [32768, 768], P(('ctx', 'head')), may hold values from -7 to 7, as said below
- values: float32 [32768, 768], P(('ctx', 'head')), may hold values from -6 to 6
- grad_out: float32 [32768, 768], P(('ctx', 'head')), may hold values from -6 to 6
- neighbours: int32 [256, 2], replicated, may hold values from 0 to 255, as said below
- bias_index: int32 [256, 3], P('ctx'), may hold values from 0 to 15
- bias_table: float32 [16, 128, 128], replicated, may hold values from -6 to 6
- head_gain: float32 [16], P('head'), may hold values from 0.5 to 2
Outputs:
- attended: float32 [32768, 768], P(('ctx', 'head'))
- grad_queries: float32 [32768, 768], P(('ctx', 'head'))
- grad_keys: float32 [32768, 768], P(('ctx', 'head'))
- grad_values: float32 [32768, 768], P(('ctx', 'head'))
- grad_table: float32 [16, 128, 128], replicated
- grad_gain: float32 [16], P('head')
Inputs may be any that keep to these rules, and one draw needn't show every extreme that they name: `neighbours`: each entry names a block of another ctx shard (entry // 8 differs from the query block's b // 8). Among the rows of one ctx shard, at most 1 entries name blocks of one other shard, and at most 1 distinct blocks of it; both bounds are reached in every draw. `queries`: entries have magnitude at most 280. `keys`: entries have magnitude at most 7.
All inputs are finite; a program needn't handle non-finite values.
Results may differ from a plain program's by a relative error of at most 0.0003.
Values sent between devices are 32-bit elements; how exact they have to be, the bound alone decides.
A program may use at most 128 MiB of HBM per device.

v0:
```python
from functools import partial
import jax
import jax.numpy as jnp
from jax import lax
from jax.sharding import PartitionSpec as P

BLOCK = 128
NEI = 2


def attend(query_block, key_sets, value_sets, edge_bias, head_gain):
    head_count = head_gain.shape[0]
    block_rows = query_block.shape[0]
    set_blocks = key_sets.shape[0]
    query_heads = query_block.reshape(block_rows, head_count, -1)
    key_heads = key_sets.reshape(set_blocks, block_rows, head_count, -1)
    value_heads = value_sets.reshape(set_blocks * block_rows, head_count, -1)
    factor = query_heads.shape[2] ** (-0.5)
    scores = (
        jnp.einsum("ihd,mchd->himc", query_heads, key_heads, precision=lax.Precision.HIGHEST)
        * factor
    )
    scores = scores + head_gain[:, None, None, None] * jnp.transpose(edge_bias, (1, 0, 2))[None]
    scores = scores.reshape(head_count, block_rows, set_blocks * block_rows)
    maxima = lax.stop_gradient(jnp.max(scores, axis=-1, keepdims=True))
    weights = jnp.exp(scores - maxima)
    weights = weights / jnp.sum(weights, axis=-1, keepdims=True)
    result = jnp.einsum("hik,khd->ihd", weights, value_heads, precision=lax.Precision.HIGHEST)
    return result.reshape(block_rows, -1)


def request_slots(requests, blocks):
    owners = requests // blocks
    ordinal = jnp.arange(requests.shape[0], dtype=jnp.int32)
    earlier = ordinal[None, :] < ordinal[:, None]
    same_owner = owners[:, None] == owners[None, :]
    return jnp.sum((same_owner & earlier).astype(jnp.int32), axis=1)


def body(queries, keys, values, grad_out, neighbours, bias_index, bias_table, head_gain):
    shards = lax.axis_size("ctx")
    myself = lax.axis_index("ctx")
    head_query, head_key, head_value, head_grad = (
        lax.all_to_all(queries, "head", split_axis=1, concat_axis=0, tiled=True),
        lax.all_to_all(keys, "head", split_axis=1, concat_axis=0, tiled=True),
        lax.all_to_all(values, "head", split_axis=1, concat_axis=0, tiled=True),
        lax.all_to_all(grad_out, "head", split_axis=1, concat_axis=0, tiled=True),
    )
    length, columns = head_query.shape
    blocks = length // BLOCK
    requests = blocks * NEI
    capacity = (requests + shards - 2) // (shards - 1)
    all_requests = neighbours.reshape(shards, requests)
    slot_all = jax.vmap(partial(request_slots, blocks=blocks))(all_requests)
    owners = all_requests // blocks
    local_ids = all_requests % blocks
    from_me = owners == myself
    slot_ids = jnp.arange(capacity, dtype=jnp.int32)
    selected = from_me[:, None, :] & (slot_all[:, None, :] == slot_ids[None, :, None])
    send_ids = jnp.max(jnp.where(selected, local_ids[:, None, :], 0), axis=2).reshape(-1)
    filled = jnp.any(selected, axis=2).reshape(-1)
    packed = jnp.concatenate([head_key, head_value], axis=1).reshape(blocks, BLOCK, 2 * columns)
    outgoing = jnp.where(filled[:, None, None], packed[send_ids], 0.0)
    arrived = lax.all_to_all(outgoing, "ctx", split_axis=0, concat_axis=0, tiled=True)
    my_owners = lax.dynamic_index_in_dim(owners, myself, 0, keepdims=False)
    my_slots = lax.dynamic_index_in_dim(slot_all, myself, 0, keepdims=False)
    wanted = my_owners * capacity + my_slots
    remote = arrived[wanted].reshape(blocks, NEI, BLOCK, 2 * columns)
    gathered = jnp.concatenate([packed[:, None], remote], axis=1)
    edge_bias = bias_table[bias_index]
    forward = jax.vmap(attend, in_axes=(0, 0, 0, 0, None))
    result, pullback = jax.vjp(
        forward,
        head_query.reshape(blocks, BLOCK, columns),
        gathered[..., :columns],
        gathered[..., columns:],
        edge_bias,
        head_gain,
    )
    query_grad, key_grad, value_grad, bias_grad, gain_grad = pullback(
        head_grad.reshape(blocks, BLOCK, columns)
    )
    attended, grad_queries = (
        lax.all_to_all(
            result.reshape(length, columns), "head", split_axis=0, concat_axis=1, tiled=True
        ),
        lax.all_to_all(
            query_grad.reshape(length, columns), "head", split_axis=0, concat_axis=1, tiled=True
        ),
    )
    remote_grad = jnp.concatenate([key_grad[:, 1:], value_grad[:, 1:]], axis=3).reshape(
        requests, BLOCK, 2 * columns
    )
    returning = (
        jnp.zeros((shards * capacity, BLOCK, 2 * columns), jnp.float32).at[wanted].add(remote_grad)
    )
    returned = lax.all_to_all(returning, "ctx", split_axis=0, concat_axis=0, tiled=True)
    local_grad = jnp.concatenate([key_grad[:, 0], value_grad[:, 0]], axis=2)
    local_grad = local_grad.at[send_ids].add(jnp.where(filled[:, None, None], returned, 0.0))
    local_grad = local_grad.reshape(length, 2 * columns)
    grad_keys, grad_values = (
        lax.all_to_all(local_grad[:, :columns], "head", split_axis=0, concat_axis=1, tiled=True),
        lax.all_to_all(local_grad[:, columns:], "head", split_axis=0, concat_axis=1, tiled=True),
    )
    table_grad = (
        jnp.zeros(bias_table.shape, jnp.float32)
        .at[bias_index.reshape(-1)]
        .add(bias_grad.reshape(-1, BLOCK, BLOCK))
    )
    grad_table = lax.psum(table_grad, ("ctx", "head"))
    grad_gain = lax.psum(gain_grad, "ctx")
    return (attended, grad_queries, grad_keys, grad_values, grad_table, grad_gain)


def solution(mesh):
    return jax.shard_map(
        body,
        mesh=mesh,
        in_specs=(
            P(("ctx", "head"), None),
            P(("ctx", "head"), None),
            P(("ctx", "head"), None),
            P(("ctx", "head"), None),
            P(),
            P("ctx", None),
            P(),
            P("head"),
        ),
        out_specs=(
            P(("ctx", "head"), None),
            P(("ctx", "head"), None),
            P(("ctx", "head"), None),
            P(("ctx", "head"), None),
            P(),
            P("head"),
        ),
        check_vma=False,
    )
```

profile of v0, /device:TPU:2, one launch (start us, length us, event | category | flops | bytes accessed | tf_op | source)
XLA Modules:
  0.0 574.3 jit_solution(18262318619627758660)
XLA Ops:
  7.2 2.0 copy.154
  9.2 4.5 all-to-all-start.1
  14.8 1.9 copy.153
  16.9 5.6 all-to-all-done.1
  22.6 3.5 all-to-all-start
  26.1 8.8 %all-to-all-done = f32[128,8,96]{0,2,1:T(8,128)S(1)} async-done(((f32[128,8,96]{0,2,1:T(8,128)}), f32[128,8,96]{0,2,1:T(8,128)S(1)}, u32[]{:S(2)}, u32[]{:S(2)}) %all-to-all-start) | async-done | bytes 393248 | tf_op jit(solution)/shard_map/all_to_all | solution.py:45
  34.9 2.4 gather_fusion
  37.4 4.0 broadcast_select_fusion.1
  41.4 11.8 %all-to-all-start.2 = ((f32[32,128,192]{1,2,0:T(8,128)}), f32[32,128,192]{1,2,0:T(8,128)}, u32[]{:S(2)}, u32[]{:S(2)}) async-start(f32[32,128,192]{1,2,0:T(8,128)} %broadcast_select_fusion.1), calls=%async_computation.2 | async-start | bytes 6291456 | tf_op jit(solution)/shard_map/all_to_all | solution.py:64
  53.4 0.9 copy.167
  54.5 70.2 %all-to-all-done.2 = f32[32,128,192]{1,2,0:T(8,128)} async-done(((f32[32,128,192]{1,2,0:T(8,128)}), f32[32,128,192]{1,2,0:T(8,128)}, u32[]{:S(2)}, u32[]{:S(2)}) %all-to-all-start.2) | async-done | bytes 3145760 | tf_op jit(solution)/shard_map/all_to_all | solution.py:64
  124.7 3.5 all-to-all-start.3
  128.9 1.6 copy.170
  131.5 2.5 gather_fusion.1
  134.1 1.6 pad_maximum_fusion.2
  135.7 1.4 all-to-all-done.3
  137.0 3.5 all-to-all-start.5
  140.5 7.1 %fusion.19 = (f32[8,2,128]{2,1,0:T(2,128)S(1)}, f32[8,2,128,3,128]{2,4,3,1,0:T(8,128)S(1)}) fusion(f32[8,128,3,128]{1,3,2,0:T(8,128)} %bitcast.132, f32[2]{0:T(128)S(1)} %copy-done.21, f32[8,128,2,48,1]{1,3,4,2,0:T(8,128)} %bitcast.145, f32[8,3,128,2,48]{2,4,3,1,0:T(8,128)} %bitcast.134), kind=kOutput, calls=%fused_computation.74 | convolution fusion | flops 456128512 | bytes 6299656 | tf_op jit(solution)/shard_map/jvp(vmap(ihd,mchd->himc))/dot_general | solution.py:20
  148.8 2.0 copy.166
  150.8 3.1 reshape.372
  154.6 6.8 %fusion = (f32[8,2,128]{2,1,0:T(2,128)S(1)}, f32[8,2,384,128]{3,2,1,0:T(8,128)S(1)}) fusion(f32[8,2,128,3,128]{2,4,3,1,0:T(8,128)S(1)} %get-tuple-element.50, f32[8,2,128]{2,1,0:T(2,128)} %multiply_divide_fusion, f32[8,2,128]{2,1,0:T(2,128)S(1)} %get-tuple-element.49, f32[8,384,2,48]{1,3,2,0:T(8,128)} %reshape.372, f32[8,2,48,128]{3,2,1,0:T(8,128)S(1)} %bitcast.143), kind=kOutput, calls=%fused_computation.8 | convolution fusion | flops 456128512 | bytes 7888896 | tf_op jit(solution)/shard_map/transpose(jvp(vmap(hik,khd->ihd)))/dot_general | solution.py:28
  161.5 2.9 multiply_reduce_fusion
  164.7 1.3 copy-done.4
  166.0 5.0 convolution_bitcast_fusion
  171.0 3.3 reshape.376
  174.3 5.1 convolution_bitcast_fusion.1
  180.2 2.0 broadcast_in_dim.27
  182.2 4.1 scatter_fusion
  186.3 8.0 %all-to-all-start.7 = ((f32[32,128,192]{1,2,0:T(8,128)}), f32[32,128,192]{1,2,0:T(8,128)}, u32[]{:S(2)}, u32[]{:S(2)}) async-start(f32[32,128,192]{1,2,0:T(8,128)} %scatter_fusion), calls=%async_computation.7 | async-start | bytes 6291456 | tf_op jit(solution)/shard_map/all_to_all | solution.py:97
  194.7 1.0 copy-done.8
  195.6 5.2 fusion.20
  200.9 3.0 fusion.4
  203.9 63.0 %all-to-all-done.7 = f32[32,128,192]{1,2,0:T(8,128)} async-done(((f32[32,128,192]{1,2,0:T(8,128)}), f32[32,128,192]{1,2,0:T(8,128)}, u32[]{:S(2)}, u32[]{:S(2)}) %all-to-all-start.7) | async-done | bytes 3145760 | tf_op jit(solution)/shard_map/all_to_all | solution.py:97
  266.9 4.4 all-to-all-start.4
  271.4 4.0 broadcast_select_fusion
  275.4 5.6 scatter_fusion.1
  281.0 5.1 all-to-all-start.6
  287.8 7.2 %all-to-all-done.6 = f32[8,128,96]{1,2,0:T(8,128)S(1)} async-done(((f32[8,128,96]{1,2,0:T(8,128)}), f32[8,128,96]{1,2,0:T(8,128)S(1)}, u32[]{:S(2)}, u32[]{:S(2)}) %all-to-all-start.6) | async-done | bytes 393248 | tf_op jit(solution)/shard_map/all_to_all | solution.py:87
  295.0 3.5 all-to-all-start.8
  298.8 1.6 copy.185
  300.6 4.5 scatter_fusion.2
  305.1 1.0 copy-done.6
  306.1 1.9 copy.211
  308.0 4.7 all-to-all-start.9
  312.6 62.4 %psum.15 = f32[2]{0:T(128)} all-reduce(f32[2]{0:T(128)S(1)} %copy-done.27), channel_id=1, replica_groups=mesh['ctx'=32,'head'=8] {'ctx'}, use_global_device_ids=true, to_apply=%region_12.13 | all-reduce | flops 2 | bytes 16 | tf_op jit(solution)/shard_map/psum | solution.py:111
  377.7 0.9 copy.189
  378.7 186.3 %all-reduce.2.cloned.1.call-done = f32[16,128,128]{2,1,0:T(8,128)} async-done(((f32[16,128,128]{2,1,0:T(8,128)}), f32[16,128,128]{2,1,0:T(8,128)}) %all-reduce.2.cloned.1.call-update) | async-done | bytes 1048592 | tf_op jit(solution)/shard_map/psum | solution.py:110
  565.0 2.3 copy.217
  (107 shorter events, 11.6 us)
Async XLA Ops:
  7.2 121.0 %copy-start = (f32[16,128,128]{2,1,0:T(8,128)S(1)}, f32[16,128,128]{2,1,0:T(8,128)}, u32[]{:S(2)}) copy-start(f32[16,128,128]{2,1,0:T(8,128)} %param.14) | copy-start | bytes 3145732
  9.2 13.4 %all-to-all-start.1 = ((f32[128,8,96]{0,2,1:T(8,128)}), f32[128,8,96]{0,2,1:T(8,128)S(1)}, u32[]{:S(2)}, u32[]{:S(2)}) async-start(f32[128,8,96]{0,2,1:T(8,128)} %bitcast.3), calls=%async_computation.1 | async-start | bytes 786432 | tf_op jit(solution)/shard_map/all_to_all | solution.py:46
  16.9 20.4 %copy-start.19 = (pred[32]{0:T(512)(128)(4,1)}, pred[32]{0:T(512)(128)(4,1)S(1)}, u32[]{:S(2)}) copy-start(pred[32]{0:T(512)(128)(4,1)S(1)} %get-tuple-element.39) | copy-start | bytes 100
  22.6 12.3 %all-to-all-start = ((f32[128,8,96]{0,2,1:T(8,128)}), f32[128,8,96]{0,2,1:T(8,128)S(1)}, u32[]{:S(2)}, u32[]{:S(2)}) async-start(f32[128,8,96]{0,2,1:T(8,128)} %bitcast), calls=%async_computation | async-start | bytes 786432 | tf_op jit(solution)/shard_map/all_to_all | solution.py:45
  26.1 11.3 %copy-start.23 = (s32[32]{0:T(128)}, s32[32]{0:T(128)S(1)}, u32[]{:S(2)}) copy-start(s32[32]{0:T(128)S(1)} %fusion.14) | copy-start | bytes 388
  34.9 2.5 copy-start.13
  41.4 11.8 %copy-start.17 = (s32[8,3]{0,1:T(4,128)S(1)}, s32[8,3]{0,1:T(4,128)}, u32[]{:S(2)}) copy-start(s32[8,3]{0,1:T(4,128)} %param.13) | copy-start | bytes 292
  41.4 12.0 %copy-start.15 = (f32[128,768]{1,0:T(8,128)S(1)}, f32[128,768]{1,0:T(8,128)}, u32[]{:S(2)}) copy-start(f32[128,768]{1,0:T(8,128)} %param.8) | copy-start | bytes 1179652
  41.4 83.4 %all-to-all-start.2 = ((f32[32,128,192]{1,2,0:T(8,128)}), f32[32,128,192]{1,2,0:T(8,128)}, u32[]{:S(2)}, u32[]{:S(2)}) async-start(f32[32,128,192]{1,2,0:T(8,128)} %broadcast_select_fusion.1), calls=%async_computation.2 | async-start | bytes 6291456 | tf_op jit(solution)/shard_map/all_to_all | solution.py:64
  54.5 70.3 %copy-start.25 = (s32[16]{0:T(128)}, s32[16]{0:T(128)S(1)}, u32[]{:S(2)}) copy-start(s32[16]{0:T(128)S(1)} %fusion.15) | copy-start | bytes 196
  124.7 12.3 %all-to-all-start.3 = ((f32[128,8,96]{0,2,1:T(8,128)}), f32[128,8,96]{0,2,1:T(8,128)S(1)}, u32[]{:S(2)}, u32[]{:S(2)}) async-start(f32[128,8,96]{0,2,1:T(8,128)} %bitcast.13), calls=%async_computation.3 | async-start | bytes 786432 | tf_op jit(solution)/shard_map/all_to_all | solution.py:44
  128.9 1.7 copy-start.16
  128.9 2.6 copy-start.14
  134.0 6.5 %copy-start.21 = (f32[2]{0:T(128)S(1)}, f32[2]{0:T(128)}, u32[]{:S(2)}) copy-start(f32[2]{0:T(128)} %param.15) | copy-start | bytes 28
  137.0 3.5 copy-start.12
  137.0 17.6 %all-to-all-start.5 = ((f32[128,8,96]{0,2,1:T(8,128)}), f32[128,8,96]{0,2,1:T(8,128)S(1)}, u32[]{:S(2)}, u32[]{:S(2)}) async-start(f32[128,8,96]{0,2,1:T(8,128)} %bitcast.154), calls=%async_computation.5 | async-start | bytes 786432 | tf_op jit(solution)/shard_map/all_to_all | solution.py:47
  147.6 1.3 copy-start.11
  154.6 6.8 %copy-start.5 = (f32[8,3,128,128]{2,3,1,0:T(8,128)S(1)}, f32[8,3,128,128]{2,3,1,0:T(8,128)}, u32[]{:S(2)}) copy-start(f32[8,3,128,128]{2,3,1,0:T(8,128)} %copy.170) | copy-start | bytes 4718596
  154.6 6.9 %copy-start.22 = (f32[2]{0:T(128)S(1)}, f32[2]{0:T(128)}, u32[]{:S(2)}) copy-start(f32[2]{0:T(128)} %param.15) | copy-start | bytes 28
  164.4 1.6 copy-start.4
  164.7 9.5 %copy-start.2 = (f32[8,2,128,384]{2,3,1,0:T(8,128)}, f32[8,2,128,384]{2,3,1,0:T(8,128)S(1)}, u32[]{:S(2)}) copy-start(f32[8,2,128,384]{2,3,1,0:T(8,128)S(1)} %broadcast_multiply_fusion) | copy-start | bytes 9437188
  174.3 5.2 copy-start.10
  180.1 2.2 copy-start.26
  186.3 8.1 %copy-start.18 = (s32[8,3]{0,1:T(4,128)S(1)}, s32[8,3]{0,1:T(4,128)}, u32[]{:S(2)}) copy-start(s32[8,3]{0,1:T(4,128)} %param.13) | copy-start | bytes 292
  186.3 8.3 %slice-start = ((f32[8,3,128,96]{2,1,3,0:T(4,128)}), f32[8,1,128,96]{2,1,3,0:T(1,128)S(1)}, s32[]{:S(2)}) async-start(f32[8,3,128,96]{2,1,3,0:T(4,128)} %reshape.376), calls=%async_computation.11 | async-start | bytes 786432 | tf_op jit(solution)/shard_map/slice | solution.py:98
  186.3 80.6 %all-to-all-start.7 = ((f32[32,128,192]{1,2,0:T(8,128)}), f32[32,128,192]{1,2,0:T(8,128)}, u32[]{:S(2)}, u32[]{:S(2)}) async-start(f32[32,128,192]{1,2,0:T(8,128)} %scatter_fusion), calls=%async_computation.7 | async-start | bytes 6291456 | tf_op jit(solution)/shard_map/all_to_all | solution.py:97
  194.4 1.3 copy-start.8
  194.6 6.3 %copy-start.3 = (f32[8,2,128,384]{2,3,1,0:T(8,128)S(1)}, f32[8,2,128,384]{2,3,1,0:T(8,128)}, u32[]{:S(2)}) copy-start(f32[8,2,128,384]{2,3,1,0:T(8,128)} %copy-done.2) | copy-start | bytes 9437188
  194.6 6.3 %copy-start.7 = (f32[8,3,128,96]{2,3,1,0:T(8,128)S(1)}, f32[8,3,128,96]{2,3,1,0:T(8,128)}, u32[]{:S(2)}) copy-start(f32[8,3,128,96]{2,3,1,0:T(8,128)} %get-tuple-element.42) | copy-start | bytes 3538948
  200.9 70.5 %copy-start.20 = (pred[32]{0:T(512)(128)(4,1)S(1)}, pred[32]{0:T(512)(128)(4,1)}, u32[]{:S(2)}) copy-start(pred[32]{0:T(512)(128)(4,1)} %copy-done.19) | copy-start | bytes 100
  266.9 14.0 %all-to-all-start.4 = ((f32[8,128,96]{1,2,0:T(8,128)}), f32[8,128,96]{1,2,0:T(8,128)S(1)}, u32[]{:S(2)}, u32[]{:S(2)}) async-start(f32[8,128,96]{1,2,0:T(8,128)} %bitcast.23), calls=%async_computation.4 | async-start | bytes 786432 | tf_op jit(solution)/shard_map/all_to_all | solution.py:84
  271.4 4.0 copy-start.24
  281.0 17.6 %copy-start.9 = (f32[8,128,384]{1,2,0:T(8,128)S(1)}, f32[8,128,384]{1,2,0:T(8,128)}, u32[]{:S(2)}) copy-start(f32[8,128,384]{1,2,0:T(8,128)} %get-tuple-element.37) | copy-start | bytes 4718596
  281.0 14.0 %all-to-all-start.6 = ((f32[8,128,96]{1,2,0:T(8,128)}), f32[8,128,96]{1,2,0:T(8,128)S(1)}, u32[]{:S(2)}, u32[]{:S(2)}) async-start(f32[8,128,96]{1,2,0:T(8,128)} %bitcast.36), calls=%async_computation.6 | async-start | bytes 786432 | tf_op jit(solution)/shard_map/all_to_all | solution.py:87
  295.0 12.9 %all-to-all-start.8 = ((f32[8,128,96]{1,2,0:T(8,128)}), f32[8,128,96]{1,2,0:T(8,128)S(1)}, u32[]{:S(2)}, u32[]{:S(2)}) async-start(f32[8,128,96]{1,2,0:T(8,128)} %bitcast.129), calls=%async_computation.8 | async-start | bytes 786432 | tf_op jit(solution)/shard_map/all_to_all | solution.py:102
  298.5 266.5 %all-reduce.2.cloned.1.call-start = ((), (), s32[]{:S(2)}) async-start(), calls=%async_computation.10 | async-start | bytes 2097152 | tf_op jit(solution)/shard_map/psum | solution.py:110
  300.5 12.1 %copy-start.27 = (f32[2]{0:T(128)S(1)}, f32[2]{0:T(128)}, u32[]{:S(2)}) copy-start(f32[2]{0:T(128)} %get-tuple-element.36) | copy-start | bytes 28
  305.0 1.0 copy-start.6
  306.0 261.2 %copy-start.1 = (f32[16,128,128]{2,1,0:T(8,128)S(1)}, f32[16,128,128]{2,1,0:T(8,128)}, u32[]{:S(2)}) copy-start(f32[16,128,128]{2,1,0:T(8,128)} %param.14) | copy-start | bytes 3145732
  308.0 69.8 %all-to-all-start.9 = ((f32[8,128,96]{1,2,0:T(8,128)}), f32[8,128,96]{1,2,0:T(8,128)S(1)}, u32[]{:S(2)}, u32[]{:S(2)}) async-start(f32[8,128,96]{1,2,0:T(8,128)} %bitcast.128), calls=%async_computation.9 | async-start | bytes 786432 | tf_op jit(solution)/shard_map/all_to_all | solution.py:103
Sparse Core Ops, SparseCore 0:
  306.2 258.7 all-reduce.1
where the time goes:
time: 583 us; the launch traced here: 574 us
  waiting for transfers between devices  343 us (59%)
  blocking collectives  62.4 us (11%)
  starting transfers between devices  52.4 us (9%)
  local copies, waits for them, and re-layouts  41.1 us (7%)
  matrix products  32.2 us (6%)
  other arithmetic  28.8 us (5%)
  between operations  14.8 us (3%)
    psum x1, waiting for transfers between devices, body(): grad_table = lax.psum(table_grad, ('ctx', 'head'))  186 us
    all_to_all x1, waiting for transfers between devices, body(): lax.all_to_all(outgoing, 'ctx', split_axis=0, concat_axis=0, tiled=True)  70.2 us
    all_to_all x1, waiting for transfers between devices, body(): lax.all_to_all(returning, 'ctx', split_axis=0, concat_axis=0, tiled=True)  63 us
    psum x1, blocking collectives, body(): grad_gain = lax.psum(gain_grad, 'ctx')  62.4 us
    unnamed x69, local copies, waits for them, and re-layouts  17.6 us
    dot_general x3, matrix products, attend(): jnp.einsum('hik,khd->ihd', weights, value_heads, precision=lax.Precision....  17 us
    dot_general x3, matrix products, attend(): jnp.einsum('ihd,mchd->himc', query_heads, key_heads, precision=lax.Precis...  15.2 us
    all_to_all x1, starting transfers between devices, body(): lax.all_to_all(outgoing, 'ctx', split_axis=0, concat_axis=0, tiled=True)  11.8 us
  transfers between devices with their start and end apart: 11, of which 7 were waited for; matrix products, arithmetic and copies ran while one was open for 10% of the time, Pallas kernels for 0%

commit v1 on v0

--- a/solution.py
+++ b/solution.py
@@ -107,7 +107,9 @@
         .at[bias_index.reshape(-1)]
         .add(bias_grad.reshape(-1, BLOCK, BLOCK))
     )
-    grad_table = lax.psum(table_grad, ("ctx", "head"))
+    grad_table = table_grad
+    for mesh_axis in ("ctx", "head"):
+        grad_table = lax.psum(grad_table, mesh_axis)
     grad_gain = lax.psum(gain_grad, "ctx")
     return (attended, grad_queries, grad_keys, grad_values, grad_table, grad_gain)
 

time: 583 us -> 467 us (0.80)
  the two profiles are of different devices: /device:TPU:2 before, /device:TPU:8 now
where the time goes in v1:
time: 467 us; the launch traced here: 458 us
  waiting for transfers between devices  214 us (46%)
  blocking collectives  72.7 us (16%)
  starting transfers between devices  56.1 us (12%)
  local copies, waits for them, and re-layouts  39.5 us (8%)
  matrix products  32 us (7%)
  other arithmetic  28.8 us (6%)
  between operations  14.8 us (3%)
    all_to_all x1, waiting for transfers between devices, body(): lax.all_to_all(outgoing, 'ctx', split_axis=0, concat_axis=0, tiled=True)  72.7 us
    psum x1, blocking collectives, body(): grad_gain = lax.psum(gain_grad, 'ctx')  72.7 us
    all_to_all x1, waiting for transfers between devices, body(): lax.all_to_all(returning, 'ctx', split_axis=0, concat_axis=0, tiled=True)  64.7 us
    psum x2, waiting for transfers between devices, body(): grad_table = lax.psum(grad_table, mesh_axis)  58.3 us
    dot_general x3, matrix products, attend(): jnp.einsum('hik,khd->ihd', weights, value_heads, precision=lax.Precision....  16.8 us
    unnamed x71, local copies, waits for them, and re-layouts  16.2 us
    dot_general x3, matrix products, attend(): jnp.einsum('ihd,mchd->himc', query_heads, key_heads, precision=lax.Precis...  15.2 us
    all_to_all x1, starting transfers between devices, body(): lax.all_to_all(outgoing, 'ctx', split_axis=0, concat_axis=0, tiled=True)  10.9 us
  transfers between devices with their start and end apart: 12, of which 6 were waited for; matrix products, arithmetic and copies ran while one was open for 12% of the time, Pallas kernels for 0%

profile of v1, /device:TPU:8, one launch (start us, length us, event | category | flops | bytes accessed | tf_op | source)
XLA Modules:
  0.0 457.8 jit_solution(7410197727473687348)
XLA Ops:
  7.2 2.0 copy.154
  9.2 5.5 %all-to-all-start.1 = ((f32[128,8,96]{0,2,1:T(8,128)}), f32[128,8,96]{0,2,1:T(8,128)S(1)}, u32[]{:S(2)}, u32[]{:S(2)}) async-start(f32[128,8,96]{0,2,1:T(8,128)} %bitcast.3), calls=%async_computation.1 | async-start | bytes 786432 | tf_op jit(solution)/shard_map/all_to_all | solution.py:46
  15.8 1.9 copy.153
  18.0 4.2 all-to-all-done.1
  22.2 4.8 %all-to-all-start = ((f32[128,8,96]{0,2,1:T(8,128)}), f32[128,8,96]{0,2,1:T(8,128)S(1)}, u32[]{:S(2)}, u32[]{:S(2)}) async-start(f32[128,8,96]{0,2,1:T(8,128)} %bitcast), calls=%async_computation | async-start | bytes 786432 | tf_op jit(solution)/shard_map/all_to_all | solution.py:45
  27.1 7.4 %all-to-all-done = f32[128,8,96]{0,2,1:T(8,128)S(1)} async-done(((f32[128,8,96]{0,2,1:T(8,128)}), f32[128,8,96]{0,2,1:T(8,128)S(1)}, u32[]{:S(2)}, u32[]{:S(2)}) %all-to-all-start) | async-done | bytes 393248 | tf_op jit(solution)/shard_map/all_to_all | solution.py:45
  34.5 2.4 gather_fusion
  37.0 4.0 broadcast_select_fusion.1
  41.0 10.9 %all-to-all-start.2 = ((f32[32,128,192]{1,2,0:T(8,128)}), f32[32,128,192]{1,2,0:T(8,128)}, u32[]{:S(2)}, u32[]{:S(2)}) async-start(f32[32,128,192]{1,2,0:T(8,128)} %broadcast_select_fusion.1), calls=%async_computation.2 | async-start | bytes 6291456 | tf_op jit(solution)/shard_map/all_to_all | solution.py:64
  52.2 0.9 copy.167
  53.3 72.7 %all-to-all-done.2 = f32[32,128,192]{1,2,0:T(8,128)} async-done(((f32[32,128,192]{1,2,0:T(8,128)}), f32[32,128,192]{1,2,0:T(8,128)}, u32[]{:S(2)}, u32[]{:S(2)}) %all-to-all-start.2) | async-done | bytes 3145760 | tf_op jit(solution)/shard_map/all_to_all | solution.py:64
  126.0 4.8 %all-to-all-start.3 = ((f32[128,8,96]{0,2,1:T(8,128)}), f32[128,8,96]{0,2,1:T(8,128)S(1)}, u32[]{:S(2)}, u32[]{:S(2)}) async-start(f32[128,8,96]{0,2,1:T(8,128)} %bitcast.13), calls=%async_computation.3 | async-start | bytes 786432 | tf_op jit(solution)/shard_map/all_to_all | solution.py:44
  131.5 1.6 copy.170
  134.2 2.5 gather_fusion.1
  136.7 1.6 pad_maximum_fusion.2
  138.3 4.8 %all-to-all-start.5 = ((f32[128,8,96]{0,2,1:T(8,128)}), f32[128,8,96]{0,2,1:T(8,128)S(1)}, u32[]{:S(2)}, u32[]{:S(2)}) async-start(f32[128,8,96]{0,2,1:T(8,128)} %bitcast.154), calls=%async_computation.5 | async-start | bytes 786432 | tf_op jit(solution)/shard_map/all_to_all | solution.py:47
  143.2 7.1 %fusion.19 = (f32[8,2,128]{2,1,0:T(2,128)S(1)}, f32[8,2,128,3,128]{2,4,3,1,0:T(8,128)S(1)}) fusion(f32[8,128,3,128]{1,3,2,0:T(8,128)} %bitcast.132, f32[2]{0:T(128)S(1)} %copy-done.22, f32[8,128,2,48,1]{1,3,4,2,0:T(8,128)} %bitcast.145, f32[8,3,128,2,48]{2,4,3,1,0:T(8,128)} %bitcast.134), kind=kOutput, calls=%fused_computation.74 | convolution fusion | flops 456128512 | bytes 6299656 | tf_op jit(solution)/shard_map/jvp(vmap(ihd,mchd->himc))/dot_general | solution.py:20
  151.5 2.0 copy.166
  153.5 3.4 reshape.372
  157.5 6.8 %fusion = (f32[8,2,128]{2,1,0:T(2,128)S(1)}, f32[8,2,384,128]{3,2,1,0:T(8,128)S(1)}) fusion(f32[8,2,128,3,128]{2,4,3,1,0:T(8,128)S(1)} %get-tuple-element.50, f32[8,2,128]{2,1,0:T(2,128)} %multiply_divide_fusion, f32[8,2,128]{2,1,0:T(2,128)S(1)} %get-tuple-element.49, f32[8,384,2,48]{1,3,2,0:T(8,128)} %reshape.372, f32[8,2,48,128]{3,2,1,0:T(8,128)S(1)} %bitcast.143), kind=kOutput, calls=%fused_computation.8 | convolution fusion | flops 456128512 | bytes 7888896 | tf_op jit(solution)/shard_map/transpose(jvp(vmap(hik,khd->ihd)))/dot_general | solution.py:28
  164.3 2.9 multiply_reduce_fusion
  167.6 1.3 copy-done.4
  168.8 5.0 %convolution_bitcast_fusion = f32[8,384,2,48]{1,3,2,0:T(8,128)} fusion(f32[8,2,128,384]{2,3,1,0:T(8,128)S(1)} %get-tuple-element.41, f32[8,2,48,128]{3,2,1,0:T(8,128)S(1)} %bitcast.144), kind=kOutput, calls=%fused_computation.23 | convolution fusion | flops 452984832 | bytes 4718592 | tf_op jit(solution)/shard_map/transpose(jvp(vmap(hik,khd->ihd)))/dot_general | solution.py:28
  173.8 3.0 reshape.376
  176.9 5.1 %convolution_bitcast_fusion.1 = f32[8,3,128,2,48]{2,4,1,3,0:T(8,128)S(1)} fusion(f32[8,2,128,3,128]{2,4,3,1,0:T(8,128)S(1)} %bitcast.130, f32[8,128,2,48,1]{1,3,4,2,0:T(8,128)} %bitcast.146), kind=kOutput, calls=%fused_computation.24 | convolution fusion | flops 452984832 | bytes 4718592 | tf_op jit(solution)/shard_map/transpose(jvp(vmap(ihd,mchd->himc)))/dot_general | solution.py:20
  183.1 2.0 broadcast_in_dim.27
  185.1 4.0 scatter_fusion
  189.2 5.6 %all-to-all-start.7 = ((f32[32,128,192]{1,2,0:T(8,128)}), f32[32,128,192]{1,2,0:T(8,128)}, u32[]{:S(2)}, u32[]{:S(2)}) async-start(f32[32,128,192]{1,2,0:T(8,128)} %scatter_fusion), calls=%async_computation.7 | async-start | bytes 6291456 | tf_op jit(solution)/shard_map/all_to_all | solution.py:97
  195.2 1.6 copy.185
  197.0 4.5 scatter_fusion.2
  201.5 1.0 copy-done.6
  202.5 1.0 slice_bitcast_fusion.2
  203.6 5.0 %fusion.20 = f32[8,2,48,128]{3,2,1,0:T(8,128)} fusion(f32[8,384,2,48]{1,3,2,0:T(8,128)S(1)} %copy-done.8, f32[8,2,128,384]{2,3,1,0:T(8,128)} %copy-done.4), kind=kOutput, calls=%fused_computation.75 | convolution fusion | flops 452984832 | bytes 4718592 | tf_op jit(solution)/shard_map/jvp(vmap(hik,khd->ihd))/dot_general | solution.py:28
  208.6 3.0 fusion.4
  211.6 64.7 %all-to-all-done.7 = f32[32,128,192]{1,2,0:T(8,128)} async-done(((f32[32,128,192]{1,2,0:T(8,128)}), f32[32,128,192]{1,2,0:T(8,128)}, u32[]{:S(2)}, u32[]{:S(2)}) %all-to-all-start.7) | async-done | bytes 3145760 | tf_op jit(solution)/shard_map/all_to_all | solution.py:97
  276.3 5.1 %all-to-all-start.4 = ((f32[8,128,96]{1,2,0:T(8,128)}), f32[8,128,96]{1,2,0:T(8,128)S(1)}, u32[]{:S(2)}, u32[]{:S(2)}) async-start(f32[8,128,96]{1,2,0:T(8,128)} %bitcast.23), calls=%async_computation.4 | async-start | bytes 786432 | tf_op jit(solution)/shard_map/all_to_all | solution.py:84
  281.5 4.0 broadcast_select_fusion
  285.5 5.6 %scatter_fusion.1 = f32[8,128,192]{1,2,0:T(8,128)S(1)} fusion(f32[8,128,192]{1,2,0:T(8,128)S(1)} %pad_maximum_fusion.4, s32[32]{0:T(128)S(1)} %copy-done.25, f32[32,128,192]{1,2,0:T(8,128)} %broadcast_select_fusion), kind=kCustom, calls=%fused_computation.4 | custom fusion | flops 786432 | bytes 9437312 | tf_op jit(solution)/shard_map/scatter-add | solution.py:99
  291.1 4.8 %all-to-all-start.6 = ((f32[8,128,96]{1,2,0:T(8,128)}), f32[8,128,96]{1,2,0:T(8,128)S(1)}, u32[]{:S(2)}, u32[]{:S(2)}) async-start(f32[8,128,96]{1,2,0:T(8,128)} %bitcast.36), calls=%async_computation.6 | async-start | bytes 786432 | tf_op jit(solution)/shard_map/all_to_all | solution.py:87
  296.8 6.5 %all-to-all-done.6 = f32[8,128,96]{1,2,0:T(8,128)S(1)} async-done(((f32[8,128,96]{1,2,0:T(8,128)}), f32[8,128,96]{1,2,0:T(8,128)S(1)}, u32[]{:S(2)}, u32[]{:S(2)}) %all-to-all-start.6) | async-done | bytes 393248 | tf_op jit(solution)/shard_map/all_to_all | solution.py:87
  303.3 4.8 %all-to-all-start.8 = ((f32[8,128,96]{1,2,0:T(8,128)}), f32[8,128,96]{1,2,0:T(8,128)S(1)}, u32[]{:S(2)}, u32[]{:S(2)}) async-start(f32[8,128,96]{1,2,0:T(8,128)} %bitcast.129), calls=%async_computation.8 | async-start | bytes 786432 | tf_op jit(solution)/shard_map/all_to_all | solution.py:102
  308.1 58.3 %all-reduce.3.cloned.1.call-done = f32[16,128,128]{2,1,0:T(8,128)} async-done(((f32[16,128,128]{2,1,0:T(8,128)}), f32[16,128,128]{2,1,0:T(8,128)}) %all-reduce.3.cloned.1.call-update) | async-done | bytes 1048592 | tf_op jit(solution)/shard_map/psum | solution.py:112
  367.2 4.8 %all-to-all-start.9 = ((f32[8,128,96]{1,2,0:T(8,128)}), f32[8,128,96]{1,2,0:T(8,128)S(1)}, u32[]{:S(2)}, u32[]{:S(2)}) async-start(f32[8,128,96]{1,2,0:T(8,128)} %bitcast.128), calls=%async_computation.9 | async-start | bytes 786432 | tf_op jit(solution)/shard_map/all_to_all | solution.py:103
  372.1 72.7 %psum.23 = f32[2]{0:T(128)} all-reduce(f32[2]{0:T(128)S(1)} %copy-done.28), channel_id=1, replica_groups=mesh['ctx'=32,'head'=8] {'ctx'}, use_global_device_ids=true, to_apply=%region_13.14 | all-reduce | flops 2 | bytes 16 | tf_op jit(solution)/shard_map/psum | solution.py:113
  445.7 0.9 copy.187
  446.6 0.9 copy.188
  447.5 0.9 copy.189
  448.5 2.3 copy.218
  (112 shorter events, 10.1 us)
Async XLA Ops:
  7.2 123.7 %copy-start = (f32[16,128,128]{2,1,0:T(8,128)S(1)}, f32[16,128,128]{2,1,0:T(8,128)}, u32[]{:S(2)}) copy-start(f32[16,128,128]{2,1,0:T(8,128)} %param.14) | copy-start | bytes 3145732
  9.2 13.0 %all-to-all-start.1 = ((f32[128,8,96]{0,2,1:T(8,128)}), f32[128,8,96]{0,2,1:T(8,128)S(1)}, u32[]{:S(2)}, u32[]{:S(2)}) async-start(f32[128,8,96]{0,2,1:T(8,128)} %bitcast.3), calls=%async_computation.1 | async-start | bytes 786432 | tf_op jit(solution)/shard_map/all_to_all | solution.py:46
  18.0 19.0 %copy-start.20 = (pred[32]{0:T(512)(128)(4,1)}, pred[32]{0:T(512)(128)(4,1)S(1)}, u32[]{:S(2)}) copy-start(pred[32]{0:T(512)(128)(4,1)S(1)} %get-tuple-element.39) | copy-start | bytes 100
  22.2 12.3 %all-to-all-start = ((f32[128,8,96]{0,2,1:T(8,128)}), f32[128,8,96]{0,2,1:T(8,128)S(1)}, u32[]{:S(2)}, u32[]{:S(2)}) async-start(f32[128,8,96]{0,2,1:T(8,128)} %bitcast), calls=%async_computation | async-start | bytes 786432 | tf_op jit(solution)/shard_map/all_to_all | solution.py:45
  27.0 10.0 %copy-start.24 = (s32[32]{0:T(128)}, s32[32]{0:T(128)S(1)}, u32[]{:S(2)}) copy-start(s32[32]{0:T(128)S(1)} %fusion.14) | copy-start | bytes 388
  34.5 2.5 copy-start.14
  41.0 11.0 %copy-start.18 = (s32[8,3]{0,1:T(4,128)S(1)}, s32[8,3]{0,1:T(4,128)}, u32[]{:S(2)}) copy-start(s32[8,3]{0,1:T(4,128)} %param.13) | copy-start | bytes 292
  41.0 11.1 %copy-start.16 = (f32[128,768]{1,0:T(8,128)S(1)}, f32[128,768]{1,0:T(8,128)}, u32[]{:S(2)}) copy-start(f32[128,768]{1,0:T(8,128)} %param.8) | copy-start | bytes 1179652
  41.0 85.0 %all-to-all-start.2 = ((f32[32,128,192]{1,2,0:T(8,128)}), f32[32,128,192]{1,2,0:T(8,128)}, u32[]{:S(2)}, u32[]{:S(2)}) async-start(f32[32,128,192]{1,2,0:T(8,128)} %broadcast_select_fusion.1), calls=%async_computation.2 | async-start | bytes 6291456 | tf_op jit(solution)/shard_map/all_to_all | solution.py:64
  53.3 72.8 %copy-start.26 = (s32[16]{0:T(128)}, s32[16]{0:T(128)S(1)}, u32[]{:S(2)}) copy-start(s32[16]{0:T(128)S(1)} %fusion.15) | copy-start | bytes 196
  126.0 12.3 %all-to-all-start.3 = ((f32[128,8,96]{0,2,1:T(8,128)}), f32[128,8,96]{0,2,1:T(8,128)S(1)}, u32[]{:S(2)}, u32[]{:S(2)}) async-start(f32[128,8,96]{0,2,1:T(8,128)} %bitcast.13), calls=%async_computation.3 | async-start | bytes 786432 | tf_op jit(solution)/shard_map/all_to_all | solution.py:44
  131.5 1.7 copy-start.17
  131.5 2.6 copy-start.15
  136.7 6.5 %copy-start.22 = (f32[2]{0:T(128)S(1)}, f32[2]{0:T(128)}, u32[]{:S(2)}) copy-start(f32[2]{0:T(128)} %param.15) | copy-start | bytes 28
  138.3 4.8 %copy-start.13 = (f32[128,8,96]{0,2,1:T(8,128)}, f32[128,8,96]{0,2,1:T(8,128)S(1)}, u32[]{:S(2)}) copy-start(f32[128,8,96]{0,2,1:T(8,128)S(1)} %all-to-all-done.3) | copy-start | bytes 1179652
  138.3 19.1 %all-to-all-start.5 = ((f32[128,8,96]{0,2,1:T(8,128)}), f32[128,8,96]{0,2,1:T(8,128)S(1)}, u32[]{:S(2)}, u32[]{:S(2)}) async-start(f32[128,8,96]{0,2,1:T(8,128)} %bitcast.154), calls=%async_computation.5 | async-start | bytes 786432 | tf_op jit(solution)/shard_map/all_to_all | solution.py:47
  150.2 1.3 copy-start.12
  157.5 6.9 %copy-start.5 = (f32[8,3,128,128]{2,3,1,0:T(8,128)S(1)}, f32[8,3,128,128]{2,3,1,0:T(8,128)}, u32[]{:S(2)}) copy-start(f32[8,3,128,128]{2,3,1,0:T(8,128)} %copy.170) | copy-start | bytes 4718596
  157.5 6.9 %copy-start.23 = (f32[2]{0:T(128)S(1)}, f32[2]{0:T(128)}, u32[]{:S(2)}) copy-start(f32[2]{0:T(128)} %param.15) | copy-start | bytes 28
  167.2 1.6 copy-start.4
  167.5 9.3 %copy-start.2 = (f32[8,2,128,384]{2,3,1,0:T(8,128)}, f32[8,2,128,384]{2,3,1,0:T(8,128)S(1)}, u32[]{:S(2)}) copy-start(f32[8,2,128,384]{2,3,1,0:T(8,128)S(1)} %broadcast_multiply_fusion) | copy-start | bytes 9437188
  176.8 5.2 %copy-start.10 = (f32[8,3,128,96]{2,1,3,0:T(4,128)S(1)}, f32[8,3,128,96]{2,1,3,0:T(4,128)}, u32[]{:S(2)}) copy-start(f32[8,3,128,96]{2,1,3,0:T(4,128)} %reshape.376) | copy-start | bytes 3538948
  182.1 1.0 copy-start.11
  182.6 2.5 copy-start.27
  189.2 5.6 %copy-start.19 = (s32[8,3]{0,1:T(4,128)S(1)}, s32[8,3]{0,1:T(4,128)}, u32[]{:S(2)}) copy-start(s32[8,3]{0,1:T(4,128)} %param.13) | copy-start | bytes 292
  189.2 5.8 %copy-start.9 = (f32[8,128,384]{1,2,0:T(8,128)S(1)}, f32[8,128,384]{1,2,0:T(8,128)}, u32[]{:S(2)}) copy-start(f32[8,128,384]{1,2,0:T(8,128)} %get-tuple-element.37) | copy-start | bytes 4718596
  189.2 87.2 %all-to-all-start.7 = ((f32[32,128,192]{1,2,0:T(8,128)}), f32[32,128,192]{1,2,0:T(8,128)}, u32[]{:S(2)}, u32[]{:S(2)}) async-start(f32[32,128,192]{1,2,0:T(8,128)} %scatter_fusion), calls=%async_computation.7 | async-start | bytes 6291456 | tf_op jit(solution)/shard_map/all_to_all | solution.py:97
  194.7 171.7 %all-reduce.3.cloned.1.call-start = ((), (), s32[]{:S(2)}) async-start(), calls=%async_computation.10 | async-start | bytes 2097152 | tf_op jit(solution)/shard_map/psum | solution.py:112
  197.0 6.5 %slice-start = ((f32[8,3,128,96]{2,1,3,0:T(4,128)}), f32[8,1,128,96]{2,1,3,0:T(1,128)S(1)}, s32[]{:S(2)}) async-start(f32[8,3,128,96]{2,1,3,0:T(4,128)} %reshape.376), calls=%async_computation.12 | async-start | bytes 786432 | tf_op jit(solution)/shard_map/slice | solution.py:98
  197.0 6.6 %copy-start.8 = (f32[8,384,2,48]{1,3,2,0:T(8,128)S(1)}, f32[8,384,2,48]{1,3,2,0:T(8,128)}, u32[]{:S(2)}) copy-start(f32[8,384,2,48]{1,3,2,0:T(8,128)} %reshape.372) | copy-start | bytes 3538948
  201.5 1.0 copy-start.6
  203.5 5.1 %copy-start.3 = (f32[8,2,128,384]{2,3,1,0:T(8,128)S(1)}, f32[8,2,128,384]{2,3,1,0:T(8,128)}, u32[]{:S(2)}) copy-start(f32[8,2,128,384]{2,3,1,0:T(8,128)} %copy-done.2) | copy-start | bytes 9437188
  203.5 5.1 %copy-start.7 = (f32[8,3,128,96]{2,3,1,0:T(8,128)S(1)}, f32[8,3,128,96]{2,3,1,0:T(8,128)}, u32[]{:S(2)}) copy-start(f32[8,3,128,96]{2,3,1,0:T(8,128)} %get-tuple-element.42) | copy-start | bytes 3538948
  208.6 72.8 %copy-start.21 = (pred[32]{0:T(512)(128)(4,1)S(1)}, pred[32]{0:T(512)(128)(4,1)}, u32[]{:S(2)}) copy-start(pred[32]{0:T(512)(128)(4,1)} %copy-done.20) | copy-start | bytes 100
  276.3 14.7 %all-to-all-start.4 = ((f32[8,128,96]{1,2,0:T(8,128)}), f32[8,128,96]{1,2,0:T(8,128)S(1)}, u32[]{:S(2)}, u32[]{:S(2)}) async-start(f32[8,128,96]{1,2,0:T(8,128)} %bitcast.23), calls=%async_computation.4 | async-start | bytes 786432 | tf_op jit(solution)/shard_map/all_to_all | solution.py:84
  281.5 4.0 copy-start.25
  291.1 12.3 %all-to-all-start.6 = ((f32[8,128,96]{1,2,0:T(8,128)}), f32[8,128,96]{1,2,0:T(8,128)S(1)}, u32[]{:S(2)}, u32[]{:S(2)}) async-start(f32[8,128,96]{1,2,0:T(8,128)} %bitcast.36), calls=%async_computation.6 | async-start | bytes 786432 | tf_op jit(solution)/shard_map/all_to_all | solution.py:87
  296.0 76.1 %copy-start.28 = (f32[2]{0:T(128)S(1)}, f32[2]{0:T(128)}, u32[]{:S(2)}) copy-start(f32[2]{0:T(128)} %get-tuple-element.36) | copy-start | bytes 28
  303.3 63.9 %all-to-all-start.8 = ((f32[8,128,96]{1,2,0:T(8,128)}), f32[8,128,96]{1,2,0:T(8,128)S(1)}, u32[]{:S(2)}, u32[]{:S(2)}) async-start(f32[8,128,96]{1,2,0:T(8,128)} %bitcast.129), calls=%async_computation.8 | async-start | bytes 786432 | tf_op jit(solution)/shard_map/all_to_all | solution.py:102
  308.1 140.3 %all-reduce.5.cloned.1.call-start = ((), (), s32[]{:S(2)}) async-start(), calls=%async_computation.11 | async-start | bytes 2097152 | tf_op jit(solution)/shard_map/psum | solution.py:112
  366.4 84.3 %copy-start.1 = (f32[16,128,128]{2,1,0:T(8,128)S(1)}, f32[16,128,128]{2,1,0:T(8,128)}, u32[]{:S(2)}) copy-start(f32[16,128,128]{2,1,0:T(8,128)} %param.14) | copy-start | bytes 3145732
  367.2 80.3 %all-to-all-start.9 = ((f32[8,128,96]{1,2,0:T(8,128)}), f32[8,128,96]{1,2,0:T(8,128)S(1)}, u32[]{:S(2)}, u32[]{:S(2)}) async-start(f32[8,128,96]{1,2,0:T(8,128)} %bitcast.128), calls=%async_computation.9 | async-start | bytes 786432 | tf_op jit(solution)/shard_map/all_to_all | solution.py:103
Sparse Core Ops, SparseCore 0:
  202.6 163.7 all-reduce.2
  368.8 63.1 all-reduce.4
